TPU v7x, 512 devices: a whole 4x4x16 slice. The times are simulated.
512 devices in a mesh: blk: 32 (over z_lo, x, core), group: 16 (over y, z_hi).
Axes of the slice: x: 4, y: 4, z: 16 (z_hi: 4, z_lo: 4; z = z_hi * 4 + z_lo), core: 2. Of those that a mesh axis runs over, the one named last changes fastest.
Arguments:
- queries: bfloat16 [16, 8192, 4096], P('group', 'blk'), may hold values from -30 to 30
- passages: bfloat16 [16, 512, 4096], P('group', 'blk'), may hold values from -7 to 7
- positives: int32 [16, 8192], P('group', 'blk'), may hold values from 0 to 511
- hard_rows: bfloat16 [16, 512, 4096], P('group', 'blk'), may hold values from -6 to 6
- hard_dest: int32 [16, 512, 1], P('group', 'blk'), may hold values from 0 to 15; in each aligned block of 16 rows (0 to 15, 16 to 31, ..., all dimensions but the last counted through in order) at most 2 rows name the same one
Outputs:
- loss_rows: float32 [16, 8192], P('group', 'blk')
- d_queries: bfloat16 [16, 8192, 4096], P('group', 'blk')
- d_passages: bfloat16 [16, 512, 4096], P('group', 'blk')
- d_hard: bfloat16 [16, 512, 4096], P('group', 'blk')
Inputs may be any that keep to these rules, and one draw needn't show every extreme that they name: `hard_dest`: among the 16 hard rows of one device, at most 2 name the same group, and some device reaches 2.
All inputs are finite; a program needn't handle non-finite values.
Results may differ from a plain program's by a relative error of at most 0.0048.
Values may be sent and summed in bfloat16 or wider, within the bound.
No kernel may reach another device: no remote copies, remote signals or barrier semaphores. Data moves between devices by JAX's collectives and lax.ppermute only.
A program may use at most 64 MiB of HBM per device.

v0:
```python
import jax
import jax.numpy as jnp
from jax import lax
from jax.sharding import PartitionSpec as P


def from_behind(x, axis, by):
    count = lax.axis_size(axis)
    return lax.ppermute(x, axis, [(i, (i + by) % count) for i in range(count)])


def body(queries, passages, positives, hard_rows, hard_dest):
    query_rows = queries[0]
    own_passages = passages[0]
    targets = positives[0]
    owned_hard = hard_rows[0]
    routes = hard_dest[0, :, 0]
    groups = lax.axis_size("group")
    blocks = lax.axis_size("blk")
    blk_index = lax.axis_index("blk")
    feat_width = query_rows.shape[1]
    passage_count = own_passages.shape[0]
    hard_count = owned_hard.shape[0]
    total_rows = passage_count * blocks
    score_multiplier = feat_width ** (-0.5)
    largest_score = lax.Precision.HIGHEST
    slot_count = max(2, 2 * hard_count // groups)
    onehot_dest = (routes[:, None] == jnp.arange(groups, dtype=jnp.int32)[None, :]).astype(
        jnp.int32
    )
    ranking = jnp.sum((jnp.cumsum(onehot_dest, axis=0) - onehot_dest) * onehot_dest, axis=1)
    slot_of = routes * slot_count + ranking
    placing = (
        slot_of[None, :] == jnp.arange(groups * slot_count, dtype=jnp.int32)[:, None]
    ).astype(jnp.bfloat16)
    packed = jnp.dot(placing, owned_hard, preferred_element_type=jnp.float32).astype(jnp.bfloat16)
    packed = packed.reshape(groups, slot_count, feat_width)
    live_flags = jnp.sum(placing, axis=1).reshape(groups, slot_count)
    arrived, arrived_flags = (
        lax.all_to_all(packed, "group", split_axis=0, concat_axis=0, tiled=True),
        lax.all_to_all(live_flags, "group", split_axis=0, concat_axis=0, tiled=True),
    )
    received = arrived.reshape(groups * slot_count, feat_width)
    is_live = arrived_flags.reshape(groups * slot_count) > 0.5
    raw_hard = score_multiplier * jnp.einsum(
        "qd,hd->qh", query_rows, received, preferred_element_type=jnp.float32
    )
    negative_scores = jnp.where(is_live[None, :], raw_hard, -jnp.inf)
    hard_top = jnp.max(negative_scores, axis=1)
    received_wide = received.astype(jnp.float32)
    target_hot = (targets[:, None] == jnp.arange(total_rows, dtype=jnp.int32)[None, :]).astype(
        jnp.float32
    )
    gathered = lax.all_gather(own_passages, "blk", axis=0, tiled=True)
    in_scores = score_multiplier * jnp.einsum(
        "qd,pd->qp", query_rows, gathered, preferred_element_type=jnp.float32
    )
    run_top = jnp.maximum(jnp.max(in_scores, axis=1), hard_top)
    run_total = jnp.sum(jnp.exp(in_scores - run_top[:, None]), axis=1) + jnp.sum(
        jnp.exp(negative_scores - run_top[:, None]), axis=1
    )
    log_total = run_top + jnp.log(run_total)
    prob_in = jnp.exp(in_scores - log_total[:, None])
    hard_probability = jnp.exp(negative_scores - log_total[:, None])
    coef_in = prob_in - target_hot
    d_query = score_multiplier * (
        jnp.dot(coef_in, gathered.astype(jnp.float32), precision=largest_score)
        + jnp.dot(hard_probability, received_wide, precision=largest_score)
    )
    loss_rows = log_total - jnp.sum(in_scores * target_hot, axis=1)
    coef_round = coef_in.astype(jnp.bfloat16)

    def contrib(col_start, row_count):
        coef_cols = lax.dynamic_slice_in_dim(coef_round, col_start, row_count, 1)
        return jnp.einsum("qp,qd->pd", coef_cols, query_rows, preferred_element_type=jnp.float32)

    def owner_col(turn_index):
        return (blk_index - turn_index - 1) % blocks * passage_count

    def advance(turn_index, running):
        running = from_behind(running, "blk", 1)
        return running + contrib(owner_col(turn_index), passage_count)

    summed = lax.fori_loop(1, blocks, advance, contrib(owner_col(0), passage_count))
    d_passage = (score_multiplier * summed).astype(jnp.bfloat16)
    hard_exchange_round = hard_probability.astype(jnp.bfloat16)
    slot_grads = (
        score_multiplier
        * jnp.einsum(
            "qh,qd->hd", hard_exchange_round, query_rows, preferred_element_type=jnp.float32
        )
    ).astype(jnp.bfloat16)
    slot_grads = slot_grads.reshape(groups, slot_count, feat_width)
    returned = lax.all_to_all(slot_grads, "group", split_axis=0, concat_axis=0, tiled=True).reshape(
        groups * slot_count, feat_width
    )
    d_owned = jnp.einsum("sh,sd->hd", placing, returned, preferred_element_type=jnp.float32).astype(
        jnp.bfloat16
    )
    return (loss_rows[None], d_query.astype(jnp.bfloat16)[None], d_passage[None], d_owned[None])


def solution(mesh):
    return jax.shard_map(
        body,
        mesh=mesh,
        in_specs=(
            P("group", "blk", None),
            P("group", "blk", None),
            P("group", "blk"),
            P("group", "blk", None),
            P("group", "blk", None),
        ),
        out_specs=(
            P("group", "blk"),
            P("group", "blk", None),
            P("group", "blk", None),
            P("group", "blk", None),
        ),
        check_vma=False,
    )
```

profile of v0, /device:TPU:8, one launch (start us, length us, event | category | flops | bytes accessed | tf_op | source)
XLA Modules:
  0.0 506.8 jit_solution(9961726672704951241)
XLA Ops:
  11.0 18.2 %all-to-all-start = ((bf16[16,1,2]{2,1,0:T(2,128)(2,1)}), bf16[16,1,2]{2,1,0:T(2,128)(2,1)S(1)}, u32[]{:S(2)}, u32[]{:S(2)}) async-start(bf16[16,1,2]{2,1,0:T(2,128)(2,1)} %all_to_all.16), calls=%async_computation | async-start | bytes 16384 | tf_op jit(solution)/shard_map/all_to_all | solution.py:41
  30.4 12.1 %all-to-all-done = bf16[16,1,2]{2,1,0:T(2,128)(2,1)S(1)} async-done(((bf16[16,1,2]{2,1,0:T(2,128)(2,1)}), bf16[16,1,2]{2,1,0:T(2,128)(2,1)S(1)}, u32[]{:S(2)}, u32[]{:S(2)}) %all-to-all-start) | async-done | bytes 96 | tf_op jit(solution)/shard_map/all_to_all | solution.py:41
  42.5 4.8 all-to-all-start.1
  47.4 22.5 %all-to-all-done.1 = bf16[16,2,4096]{2,1,0:T(2,128)(2,1)S(1)} async-done(((bf16[16,2,4096]{2,1,0:T(2,128)(2,1)}), bf16[16,2,4096]{2,1,0:T(2,128)(2,1)S(1)}, u32[]{:S(2)}, u32[]{:S(2)}) %all-to-all-start.1) | async-done | bytes 262176 | tf_op jit(solution)/shard_map/all_to_all | solution.py:40
  70.9 20.0 %all-gather.3.cloned.1.call-done = bf16[1,512,4096]{2,1,0:T(8,128)(2,1)} async-done(((bf16[1,16,4096]{2,1,0:T(8,128)(2,1)}), bf16[1,512,4096]{2,1,0:T(8,128)(2,1)}) %all-gather.3.cloned.1.call-update) | async-done | bytes 4194320 | tf_op jit(solution)/shard_map/all_gather | solution.py:54
  90.9 3.7 fusion.37
  96.2 3.8 fusion.7
  100.0 3.3 fusion.4
  104.2 15.7 %all-to-all-start.2 = ((bf16[16,2,4096]{2,1,0:T(2,128)(2,1)}), bf16[16,2,4096]{2,1,0:T(2,128)(2,1)S(1)}, u32[]{:S(2)}, u32[]{:S(2)}) async-start(bf16[16,2,4096]{2,1,0:T(2,128)(2,1)} %reshape.101), calls=%async_computation.2 | async-start | bytes 524288 | tf_op jit(solution)/shard_map/all_to_all | solution.py:94
  120.4 378.0 %while.15 = (s32[]{:T(128)}, f32[16,4096]{1,0:T(8,128)S(1)}, s32[]{:T(128)}, bf16[256,512]{1,0:T(8,128)(2,1)S(1)}, bf16[256,4096]{1,0:T(8,128)(2,1)S(1)}, /*inde...) while((s32[]{:T(128)}, f32[16,4096]{1,0:T(8,128)S(1)}, ...), condition=%wide.region_9.10_spmd, body=%wide.region_8.9_spmd.sunk | while | flops 33619984 | bytes 3735892 | solution.py:84
  120.4 1.9 collective-permute-start
  122.3 12.9 %collective-permute-done = f32[16,4096]{1,0:T(8,128)S(1)} collective-permute-done((f32[16,4096]{1,0:T(8,128)S(1)}, f32[16,4096]{1,0:T(8,128)S(1)}, u32[]{:S(2)}, u32[]{:S(2)}) %collective-permute-start) | collective-permute-done | bytes 262176 | tf_op jit(solution)/shard_map/while/body/eval_jaxpr/ppermute | solution.py:9
  137.7 10.0 %collective-permute-done = f32[16,4096]{1,0:T(8,128)S(1)} collective-permute-done((f32[16,4096]{1,0:T(8,128)S(1)}, f32[16,4096]{1,0:T(8,128)S(1)}, u32[]{:S(2)}, u32[]{:S(2)}) %collective-permute-start) | collective-permute-done | bytes 262176 | tf_op jit(solution)/shard_map/while/body/eval_jaxpr/ppermute | solution.py:9
  148.2 1.9 collective-permute-start
  150.1 9.6 %collective-permute-done = f32[16,4096]{1,0:T(8,128)S(1)} collective-permute-done((f32[16,4096]{1,0:T(8,128)S(1)}, f32[16,4096]{1,0:T(8,128)S(1)}, u32[]{:S(2)}, u32[]{:S(2)}) %collective-permute-start) | collective-permute-done | bytes 262176 | tf_op jit(solution)/shard_map/while/body/eval_jaxpr/ppermute | solution.py:9
  162.2 9.6 %collective-permute-done = f32[16,4096]{1,0:T(8,128)S(1)} collective-permute-done((f32[16,4096]{1,0:T(8,128)S(1)}, f32[16,4096]{1,0:T(8,128)S(1)}, u32[]{:S(2)}, u32[]{:S(2)}) %collective-permute-start) | collective-permute-done | bytes 262176 | tf_op jit(solution)/shard_map/while/body/eval_jaxpr/ppermute | solution.py:9
  172.3 1.9 collective-permute-start
  174.3 9.6 %collective-permute-done = f32[16,4096]{1,0:T(8,128)S(1)} collective-permute-done((f32[16,4096]{1,0:T(8,128)S(1)}, f32[16,4096]{1,0:T(8,128)S(1)}, u32[]{:S(2)}, u32[]{:S(2)}) %collective-permute-start) | collective-permute-done | bytes 262176 | tf_op jit(solution)/shard_map/while/body/eval_jaxpr/ppermute | solution.py:9
  184.4 1.9 collective-permute-start
  186.3 9.6 %collective-permute-done = f32[16,4096]{1,0:T(8,128)S(1)} collective-permute-done((f32[16,4096]{1,0:T(8,128)S(1)}, f32[16,4096]{1,0:T(8,128)S(1)}, u32[]{:S(2)}, u32[]{:S(2)}) %collective-permute-start) | collective-permute-done | bytes 262176 | tf_op jit(solution)/shard_map/while/body/eval_jaxpr/ppermute | solution.py:9
  196.5 1.9 collective-permute-start
  198.4 9.6 %collective-permute-done = f32[16,4096]{1,0:T(8,128)S(1)} collective-permute-done((f32[16,4096]{1,0:T(8,128)S(1)}, f32[16,4096]{1,0:T(8,128)S(1)}, u32[]{:S(2)}, u32[]{:S(2)}) %collective-permute-start) | collective-permute-done | bytes 262176 | tf_op jit(solution)/shard_map/while/body/eval_jaxpr/ppermute | solution.py:9
  208.5 1.9 collective-permute-start
  210.5 9.6 %collective-permute-done = f32[16,4096]{1,0:T(8,128)S(1)} collective-permute-done((f32[16,4096]{1,0:T(8,128)S(1)}, f32[16,4096]{1,0:T(8,128)S(1)}, u32[]{:S(2)}, u32[]{:S(2)}) %collective-permute-start) | collective-permute-done | bytes 262176 | tf_op jit(solution)/shard_map/while/body/eval_jaxpr/ppermute | solution.py:9
  220.6 1.9 collective-permute-start
  222.6 9.6 %collective-permute-done = f32[16,4096]{1,0:T(8,128)S(1)} collective-permute-done((f32[16,4096]{1,0:T(8,128)S(1)}, f32[16,4096]{1,0:T(8,128)S(1)}, u32[]{:S(2)}, u32[]{:S(2)}) %collective-permute-start) | collective-permute-done | bytes 262176 | tf_op jit(solution)/shard_map/while/body/eval_jaxpr/ppermute | solution.py:9
  234.6 9.6 %collective-permute-done = f32[16,4096]{1,0:T(8,128)S(1)} collective-permute-done((f32[16,4096]{1,0:T(8,128)S(1)}, f32[16,4096]{1,0:T(8,128)S(1)}, u32[]{:S(2)}, u32[]{:S(2)}) %collective-permute-start) | collective-permute-done | bytes 262176 | tf_op jit(solution)/shard_map/while/body/eval_jaxpr/ppermute | solution.py:9
  246.7 9.6 %collective-permute-done = f32[16,4096]{1,0:T(8,128)S(1)} collective-permute-done((f32[16,4096]{1,0:T(8,128)S(1)}, f32[16,4096]{1,0:T(8,128)S(1)}, u32[]{:S(2)}, u32[]{:S(2)}) %collective-permute-start) | collective-permute-done | bytes 262176 | tf_op jit(solution)/shard_map/while/body/eval_jaxpr/ppermute | solution.py:9
  258.8 9.6 %collective-permute-done = f32[16,4096]{1,0:T(8,128)S(1)} collective-permute-done((f32[16,4096]{1,0:T(8,128)S(1)}, f32[16,4096]{1,0:T(8,128)S(1)}, u32[]{:S(2)}, u32[]{:S(2)}) %collective-permute-start) | collective-permute-done | bytes 262176 | tf_op jit(solution)/shard_map/while/body/eval_jaxpr/ppermute | solution.py:9
  270.9 9.6 %collective-permute-done = f32[16,4096]{1,0:T(8,128)S(1)} collective-permute-done((f32[16,4096]{1,0:T(8,128)S(1)}, f32[16,4096]{1,0:T(8,128)S(1)}, u32[]{:S(2)}, u32[]{:S(2)}) %collective-permute-start) | collective-permute-done | bytes 262176 | tf_op jit(solution)/shard_map/while/body/eval_jaxpr/ppermute | solution.py:9
  282.9 9.6 %collective-permute-done = f32[16,4096]{1,0:T(8,128)S(1)} collective-permute-done((f32[16,4096]{1,0:T(8,128)S(1)}, f32[16,4096]{1,0:T(8,128)S(1)}, u32[]{:S(2)}, u32[]{:S(2)}) %collective-permute-start) | collective-permute-done | bytes 262176 | tf_op jit(solution)/shard_map/while/body/eval_jaxpr/ppermute | solution.py:9
  295.0 9.6 %collective-permute-done = f32[16,4096]{1,0:T(8,128)S(1)} collective-permute-done((f32[16,4096]{1,0:T(8,128)S(1)}, f32[16,4096]{1,0:T(8,128)S(1)}, u32[]{:S(2)}, u32[]{:S(2)}) %collective-permute-start) | collective-permute-done | bytes 262176 | tf_op jit(solution)/shard_map/while/body/eval_jaxpr/ppermute | solution.py:9
  307.1 9.6 %collective-permute-done = f32[16,4096]{1,0:T(8,128)S(1)} collective-permute-done((f32[16,4096]{1,0:T(8,128)S(1)}, f32[16,4096]{1,0:T(8,128)S(1)}, u32[]{:S(2)}, u32[]{:S(2)}) %collective-permute-start) | collective-permute-done | bytes 262176 | tf_op jit(solution)/shard_map/while/body/eval_jaxpr/ppermute | solution.py:9
  319.2 9.6 %collective-permute-done = f32[16,4096]{1,0:T(8,128)S(1)} collective-permute-done((f32[16,4096]{1,0:T(8,128)S(1)}, f32[16,4096]{1,0:T(8,128)S(1)}, u32[]{:S(2)}, u32[]{:S(2)}) %collective-permute-start) | collective-permute-done | bytes 262176 | tf_op jit(solution)/shard_map/while/body/eval_jaxpr/ppermute | solution.py:9
  331.2 9.6 %collective-permute-done = f32[16,4096]{1,0:T(8,128)S(1)} collective-permute-done((f32[16,4096]{1,0:T(8,128)S(1)}, f32[16,4096]{1,0:T(8,128)S(1)}, u32[]{:S(2)}, u32[]{:S(2)}) %collective-permute-start) | collective-permute-done | bytes 262176 | tf_op jit(solution)/shard_map/while/body/eval_jaxpr/ppermute | solution.py:9
  343.3 9.6 %collective-permute-done = f32[16,4096]{1,0:T(8,128)S(1)} collective-permute-done((f32[16,4096]{1,0:T(8,128)S(1)}, f32[16,4096]{1,0:T(8,128)S(1)}, u32[]{:S(2)}, u32[]{:S(2)}) %collective-permute-start) | collective-permute-done | bytes 262176 | tf_op jit(solution)/shard_map/while/body/eval_jaxpr/ppermute | solution.py:9
  355.4 9.6 %collective-permute-done = f32[16,4096]{1,0:T(8,128)S(1)} collective-permute-done((f32[16,4096]{1,0:T(8,128)S(1)}, f32[16,4096]{1,0:T(8,128)S(1)}, u32[]{:S(2)}, u32[]{:S(2)}) %collective-permute-start) | collective-permute-done | bytes 262176 | tf_op jit(solution)/shard_map/while/body/eval_jaxpr/ppermute | solution.py:9
  367.5 9.6 %collective-permute-done = f32[16,4096]{1,0:T(8,128)S(1)} collective-permute-done((f32[16,4096]{1,0:T(8,128)S(1)}, f32[16,4096]{1,0:T(8,128)S(1)}, u32[]{:S(2)}, u32[]{:S(2)}) %collective-permute-start) | collective-permute-done | bytes 262176 | tf_op jit(solution)/shard_map/while/body/eval_jaxpr/ppermute | solution.py:9
  379.5 9.6 %collective-permute-done = f32[16,4096]{1,0:T(8,128)S(1)} collective-permute-done((f32[16,4096]{1,0:T(8,128)S(1)}, f32[16,4096]{1,0:T(8,128)S(1)}, u32[]{:S(2)}, u32[]{:S(2)}) %collective-permute-start) | collective-permute-done | bytes 262176 | tf_op jit(solution)/shard_map/while/body/eval_jaxpr/ppermute | solution.py:9
  391.6 9.6 %collective-permute-done = f32[16,4096]{1,0:T(8,128)S(1)} collective-permute-done((f32[16,4096]{1,0:T(8,128)S(1)}, f32[16,4096]{1,0:T(8,128)S(1)}, u32[]{:S(2)}, u32[]{:S(2)}) %collective-permute-start) | collective-permute-done | bytes 262176 | tf_op jit(solution)/shard_map/while/body/eval_jaxpr/ppermute | solution.py:9
  403.7 9.6 %collective-permute-done = f32[16,4096]{1,0:T(8,128)S(1)} collective-permute-done((f32[16,4096]{1,0:T(8,128)S(1)}, f32[16,4096]{1,0:T(8,128)S(1)}, u32[]{:S(2)}, u32[]{:S(2)}) %collective-permute-start) | collective-permute-done | bytes 262176 | tf_op jit(solution)/shard_map/while/body/eval_jaxpr/ppermute | solution.py:9
  415.8 9.6 %collective-permute-done = f32[16,4096]{1,0:T(8,128)S(1)} collective-permute-done((f32[16,4096]{1,0:T(8,128)S(1)}, f32[16,4096]{1,0:T(8,128)S(1)}, u32[]{:S(2)}, u32[]{:S(2)}) %collective-permute-start) | collective-permute-done | bytes 262176 | tf_op jit(solution)/shard_map/while/body/eval_jaxpr/ppermute | solution.py:9
  427.8 9.6 %collective-permute-done = f32[16,4096]{1,0:T(8,128)S(1)} collective-permute-done((f32[16,4096]{1,0:T(8,128)S(1)}, f32[16,4096]{1,0:T(8,128)S(1)}, u32[]{:S(2)}, u32[]{:S(2)}) %collective-permute-start) | collective-permute-done | bytes 262176 | tf_op jit(solution)/shard_map/while/body/eval_jaxpr/ppermute | solution.py:9
  439.9 9.6 %collective-permute-done = f32[16,4096]{1,0:T(8,128)S(1)} collective-permute-done((f32[16,4096]{1,0:T(8,128)S(1)}, f32[16,4096]{1,0:T(8,128)S(1)}, u32[]{:S(2)}, u32[]{:S(2)}) %collective-permute-start) | collective-permute-done | bytes 262176 | tf_op jit(solution)/shard_map/while/body/eval_jaxpr/ppermute | solution.py:9
  452.0 9.6 %collective-permute-done = f32[16,4096]{1,0:T(8,128)S(1)} collective-permute-done((f32[16,4096]{1,0:T(8,128)S(1)}, f32[16,4096]{1,0:T(8,128)S(1)}, u32[]{:S(2)}, u32[]{:S(2)}) %collective-permute-start) | collective-permute-done | bytes 262176 | tf_op jit(solution)/shard_map/while/body/eval_jaxpr/ppermute | solution.py:9
  464.1 9.6 %collective-permute-done = f32[16,4096]{1,0:T(8,128)S(1)} collective-permute-done((f32[16,4096]{1,0:T(8,128)S(1)}, f32[16,4096]{1,0:T(8,128)S(1)}, u32[]{:S(2)}, u32[]{:S(2)}) %collective-permute-start) | collective-permute-done | bytes 262176 | tf_op jit(solution)/shard_map/while/body/eval_jaxpr/ppermute | solution.py:9
  476.1 9.6 %collective-permute-done = f32[16,4096]{1,0:T(8,128)S(1)} collective-permute-done((f32[16,4096]{1,0:T(8,128)S(1)}, f32[16,4096]{1,0:T(8,128)S(1)}, u32[]{:S(2)}, u32[]{:S(2)}) %collective-permute-start) | collective-permute-done | bytes 262176 | tf_op jit(solution)/shard_map/while/body/eval_jaxpr/ppermute | solution.py:9
  488.2 9.6 %collective-permute-done = f32[16,4096]{1,0:T(8,128)S(1)} collective-permute-done((f32[16,4096]{1,0:T(8,128)S(1)}, f32[16,4096]{1,0:T(8,128)S(1)}, u32[]{:S(2)}, u32[]{:S(2)}) %collective-permute-start) | collective-permute-done | bytes 262176 | tf_op jit(solution)/shard_map/while/body/eval_jaxpr/ppermute | solution.py:9
  (89 shorter events, 71.5 us)
Async XLA Ops:
  7.2 22.0 %copy-start = (bf16[1,16,4096]{2,1,0:T(8,128)(2,1)S(1)}, bf16[1,16,4096]{2,1,0:T(8,128)(2,1)}, u32[]{:S(2)}) copy-start(bf16[1,16,4096]{2,1,0:T(8,128)(2,1)} %param.10) | copy-start | bytes 393220
  7.2 62.9 %copy-start.1 = (bf16[1,256,4096]{2,1,0:T(8,128)(2,1)S(1)}, bf16[1,256,4096]{2,1,0:T(8,128)(2,1)}, u32[]{:S(2)}) copy-start(bf16[1,256,4096]{2,1,0:T(8,128)(2,1)} %param.7) | copy-start | bytes 6291460
  7.2 83.7 %all-gather.3.cloned.1.call-start = ((), (), s32[]{:S(2)}) async-start(), calls=%async_computation.3 | async-start | bytes 4325376 | tf_op jit(solution)/shard_map/all_gather | solution.py:54
  11.0 31.5 %all-to-all-start = ((bf16[16,1,2]{2,1,0:T(2,128)(2,1)}), bf16[16,1,2]{2,1,0:T(2,128)(2,1)S(1)}, u32[]{:S(2)}, u32[]{:S(2)}) async-start(bf16[16,1,2]{2,1,0:T(2,128)(2,1)} %all_to_all.16), calls=%async_computation | async-start | bytes 16384 | tf_op jit(solution)/shard_map/all_to_all | solution.py:41
  42.5 27.5 %all-to-all-start.1 = ((bf16[16,2,4096]{2,1,0:T(2,128)(2,1)}), bf16[16,2,4096]{2,1,0:T(2,128)(2,1)S(1)}, u32[]{:S(2)}, u32[]{:S(2)}) async-start(bf16[16,2,4096]{2,1,0:T(2,128)(2,1)} %reshape.99), calls=%async_computation.1 | async-start | bytes 524288 | tf_op jit(solution)/shard_map/all_to_all | solution.py:40
  70.8 23.8 %copy-start.3 = (s32[1,256]{1,0:T(1,128)S(1)}, s32[1,256]{1,0:T(1,128)}, u32[]{:S(2)}) copy-start(s32[1,256]{1,0:T(1,128)} %param.9) | copy-start | bytes 3076
  90.9 5.3 %copy-start.2 = (bf16[1,512,4096]{2,1,0:T(8,128)(2,1)S(1)}, bf16[1,512,4096]{2,1,0:T(8,128)(2,1)}, u32[]{:S(2)}) copy-start(bf16[1,512,4096]{2,1,0:T(8,128)(2,1)} %all-gather.3.cloned.1.call-done) | copy-start | bytes 12582916
  104.2 394.8 %all-to-all-start.2 = ((bf16[16,2,4096]{2,1,0:T(2,128)(2,1)}), bf16[16,2,4096]{2,1,0:T(2,128)(2,1)S(1)}, u32[]{:S(2)}, u32[]{:S(2)}) async-start(bf16[16,2,4096]{2,1,0:T(2,128)(2,1)} %reshape.101), calls=%async_computation.2 | async-start | bytes 524288 | tf_op jit(solution)/shard_map/all_to_all | solution.py:94
  120.4 14.9 %collective-permute-start = (f32[16,4096]{1,0:T(8,128)S(1)}, f32[16,4096]{1,0:T(8,128)S(1)}, u32[]{:S(2)}, u32[]{:S(2)}) collective-permute-start(f32[16,4096]{1,0:T(8,128)S(1)} %get-tuple-element.201), channel_id=1, source_target_pairs={{0,16},{16,32},{32,48},{48,64},{64,80},{80,96},{96,112},{112,128},... | collective-permute-start | bytes 786440 | tf_op jit(solution)/shard_map/while/body/eval_jaxpr/ppermute | solution.py:9
  135.7 11.9 %collective-permute-start = (f32[16,4096]{1,0:T(8,128)S(1)}, f32[16,4096]{1,0:T(8,128)S(1)}, u32[]{:S(2)}, u32[]{:S(2)}) collective-permute-start(f32[16,4096]{1,0:T(8,128)S(1)} %get-tuple-element.201), channel_id=1, source_target_pairs={{0,16},{16,32},{32,48},{48,64},{64,80},{80,96},{96,112},{112,128},... | collective-permute-start | bytes 786440 | tf_op jit(solution)/shard_map/while/body/eval_jaxpr/ppermute | solution.py:9
  148.2 11.6 %collective-permute-start = (f32[16,4096]{1,0:T(8,128)S(1)}, f32[16,4096]{1,0:T(8,128)S(1)}, u32[]{:S(2)}, u32[]{:S(2)}) collective-permute-start(f32[16,4096]{1,0:T(8,128)S(1)} %get-tuple-element.201), channel_id=1, source_target_pairs={{0,16},{16,32},{32,48},{48,64},{64,80},{80,96},{96,112},{112,128},... | collective-permute-start | bytes 786440 | tf_op jit(solution)/shard_map/while/body/eval_jaxpr/ppermute | solution.py:9
  160.2 11.6 %collective-permute-start = (f32[16,4096]{1,0:T(8,128)S(1)}, f32[16,4096]{1,0:T(8,128)S(1)}, u32[]{:S(2)}, u32[]{:S(2)}) collective-permute-start(f32[16,4096]{1,0:T(8,128)S(1)} %get-tuple-element.201), channel_id=1, source_target_pairs={{0,16},{16,32},{32,48},{48,64},{64,80},{80,96},{96,112},{112,128},... | collective-permute-start | bytes 786440 | tf_op jit(solution)/shard_map/while/body/eval_jaxpr/ppermute | solution.py:9
  172.3 11.6 %collective-permute-start = (f32[16,4096]{1,0:T(8,128)S(1)}, f32[16,4096]{1,0:T(8,128)S(1)}, u32[]{:S(2)}, u32[]{:S(2)}) collective-permute-start(f32[16,4096]{1,0:T(8,128)S(1)} %get-tuple-element.201), channel_id=1, source_target_pairs={{0,16},{16,32},{32,48},{48,64},{64,80},{80,96},{96,112},{112,128},... | collective-permute-start | bytes 786440 | tf_op jit(solution)/shard_map/while/body/eval_jaxpr/ppermute | solution.py:9
  184.4 11.6 %collective-permute-start = (f32[16,4096]{1,0:T(8,128)S(1)}, f32[16,4096]{1,0:T(8,128)S(1)}, u32[]{:S(2)}, u32[]{:S(2)}) collective-permute-start(f32[16,4096]{1,0:T(8,128)S(1)} %get-tuple-element.201), channel_id=1, source_target_pairs={{0,16},{16,32},{32,48},{48,64},{64,80},{80,96},{96,112},{112,128},... | collective-permute-start | bytes 786440 | tf_op jit(solution)/shard_map/while/body/eval_jaxpr/ppermute | solution.py:9
  196.5 11.6 %collective-permute-start = (f32[16,4096]{1,0:T(8,128)S(1)}, f32[16,4096]{1,0:T(8,128)S(1)}, u32[]{:S(2)}, u32[]{:S(2)}) collective-permute-start(f32[16,4096]{1,0:T(8,128)S(1)} %get-tuple-element.201), channel_id=1, source_target_pairs={{0,16},{16,32},{32,48},{48,64},{64,80},{80,96},{96,112},{112,128},... | collective-permute-start | bytes 786440 | tf_op jit(solution)/shard_map/while/body/eval_jaxpr/ppermute | solution.py:9
  208.5 11.6 %collective-permute-start = (f32[16,4096]{1,0:T(8,128)S(1)}, f32[16,4096]{1,0:T(8,128)S(1)}, u32[]{:S(2)}, u32[]{:S(2)}) collective-permute-start(f32[16,4096]{1,0:T(8,128)S(1)} %get-tuple-element.201), channel_id=1, source_target_pairs={{0,16},{16,32},{32,48},{48,64},{64,80},{80,96},{96,112},{112,128},... | collective-permute-start | bytes 786440 | tf_op jit(solution)/shard_map/while/body/eval_jaxpr/ppermute | solution.py:9
  220.6 11.6 %collective-permute-start = (f32[16,4096]{1,0:T(8,128)S(1)}, f32[16,4096]{1,0:T(8,128)S(1)}, u32[]{:S(2)}, u32[]{:S(2)}) collective-permute-start(f32[16,4096]{1,0:T(8,128)S(1)} %get-tuple-element.201), channel_id=1, source_target_pairs={{0,16},{16,32},{32,48},{48,64},{64,80},{80,96},{96,112},{112,128},... | collective-permute-start | bytes 786440 | tf_op jit(solution)/shard_map/while/body/eval_jaxpr/ppermute | solution.py:9
  232.7 11.6 %collective-permute-start = (f32[16,4096]{1,0:T(8,128)S(1)}, f32[16,4096]{1,0:T(8,128)S(1)}, u32[]{:S(2)}, u32[]{:S(2)}) collective-permute-start(f32[16,4096]{1,0:T(8,128)S(1)} %get-tuple-element.201), channel_id=1, source_target_pairs={{0,16},{16,32},{32,48},{48,64},{64,80},{80,96},{96,112},{112,128},... | collective-permute-start | bytes 786440 | tf_op jit(solution)/shard_map/while/body/eval_jaxpr/ppermute | solution.py:9
  244.8 11.6 %collective-permute-start = (f32[16,4096]{1,0:T(8,128)S(1)}, f32[16,4096]{1,0:T(8,128)S(1)}, u32[]{:S(2)}, u32[]{:S(2)}) collective-permute-start(f32[16,4096]{1,0:T(8,128)S(1)} %get-tuple-element.201), channel_id=1, source_target_pairs={{0,16},{16,32},{32,48},{48,64},{64,80},{80,96},{96,112},{112,128},... | collective-permute-start | bytes 786440 | tf_op jit(solution)/shard_map/while/body/eval_jaxpr/ppermute | solution.py:9
  256.8 11.6 %collective-permute-start = (f32[16,4096]{1,0:T(8,128)S(1)}, f32[16,4096]{1,0:T(8,128)S(1)}, u32[]{:S(2)}, u32[]{:S(2)}) collective-permute-start(f32[16,4096]{1,0:T(8,128)S(1)} %get-tuple-element.201), channel_id=1, source_target_pairs={{0,16},{16,32},{32,48},{48,64},{64,80},{80,96},{96,112},{112,128},... | collective-permute-start | bytes 786440 | tf_op jit(solution)/shard_map/while/body/eval_jaxpr/ppermute | solution.py:9
  268.9 11.6 %collective-permute-start = (f32[16,4096]{1,0:T(8,128)S(1)}, f32[16,4096]{1,0:T(8,128)S(1)}, u32[]{:S(2)}, u32[]{:S(2)}) collective-permute-start(f32[16,4096]{1,0:T(8,128)S(1)} %get-tuple-element.201), channel_id=1, source_target_pairs={{0,16},{16,32},{32,48},{48,64},{64,80},{80,96},{96,112},{112,128},... | collective-permute-start | bytes 786440 | tf_op jit(solution)/shard_map/while/body/eval_jaxpr/ppermute | solution.py:9
  281.0 11.6 %collective-permute-start = (f32[16,4096]{1,0:T(8,128)S(1)}, f32[16,4096]{1,0:T(8,128)S(1)}, u32[]{:S(2)}, u32[]{:S(2)}) collective-permute-start(f32[16,4096]{1,0:T(8,128)S(1)} %get-tuple-element.201), channel_id=1, source_target_pairs={{0,16},{16,32},{32,48},{48,64},{64,80},{80,96},{96,112},{112,128},... | collective-permute-start | bytes 786440 | tf_op jit(solution)/shard_map/while/body/eval_jaxpr/ppermute | solution.py:9
  293.1 11.6 %collective-permute-start = (f32[16,4096]{1,0:T(8,128)S(1)}, f32[16,4096]{1,0:T(8,128)S(1)}, u32[]{:S(2)}, u32[]{:S(2)}) collective-permute-start(f32[16,4096]{1,0:T(8,128)S(1)} %get-tuple-element.201), channel_id=1, source_target_pairs={{0,16},{16,32},{32,48},{48,64},{64,80},{80,96},{96,112},{112,128},... | collective-permute-start | bytes 786440 | tf_op jit(solution)/shard_map/while/body/eval_jaxpr/ppermute | solution.py:9
  305.1 11.6 %collective-permute-start = (f32[16,4096]{1,0:T(8,128)S(1)}, f32[16,4096]{1,0:T(8,128)S(1)}, u32[]{:S(2)}, u32[]{:S(2)}) collective-permute-start(f32[16,4096]{1,0:T(8,128)S(1)} %get-tuple-element.201), channel_id=1, source_target_pairs={{0,16},{16,32},{32,48},{48,64},{64,80},{80,96},{96,112},{112,128},... | collective-permute-start | bytes 786440 | tf_op jit(solution)/shard_map/while/body/eval_jaxpr/ppermute | solution.py:9
  317.2 11.6 %collective-permute-start = (f32[16,4096]{1,0:T(8,128)S(1)}, f32[16,4096]{1,0:T(8,128)S(1)}, u32[]{:S(2)}, u32[]{:S(2)}) collective-permute-start(f32[16,4096]{1,0:T(8,128)S(1)} %get-tuple-element.201), channel_id=1, source_target_pairs={{0,16},{16,32},{32,48},{48,64},{64,80},{80,96},{96,112},{112,128},... | collective-permute-start | bytes 786440 | tf_op jit(solution)/shard_map/while/body/eval_jaxpr/ppermute | solution.py:9
  329.3 11.6 %collective-permute-start = (f32[16,4096]{1,0:T(8,128)S(1)}, f32[16,4096]{1,0:T(8,128)S(1)}, u32[]{:S(2)}, u32[]{:S(2)}) collective-permute-start(f32[16,4096]{1,0:T(8,128)S(1)} %get-tuple-element.201), channel_id=1, source_target_pairs={{0,16},{16,32},{32,48},{48,64},{64,80},{80,96},{96,112},{112,128},... | collective-permute-start | bytes 786440 | tf_op jit(solution)/shard_map/while/body/eval_jaxpr/ppermute | solution.py:9
  341.4 11.6 %collective-permute-start = (f32[16,4096]{1,0:T(8,128)S(1)}, f32[16,4096]{1,0:T(8,128)S(1)}, u32[]{:S(2)}, u32[]{:S(2)}) collective-permute-start(f32[16,4096]{1,0:T(8,128)S(1)} %get-tuple-element.201), channel_id=1, source_target_pairs={{0,16},{16,32},{32,48},{48,64},{64,80},{80,96},{96,112},{112,128},... | collective-permute-start | bytes 786440 | tf_op jit(solution)/shard_map/while/body/eval_jaxpr/ppermute | solution.py:9
  353.4 11.6 %collective-permute-start = (f32[16,4096]{1,0:T(8,128)S(1)}, f32[16,4096]{1,0:T(8,128)S(1)}, u32[]{:S(2)}, u32[]{:S(2)}) collective-permute-start(f32[16,4096]{1,0:T(8,128)S(1)} %get-tuple-element.201), channel_id=1, source_target_pairs={{0,16},{16,32},{32,48},{48,64},{64,80},{80,96},{96,112},{112,128},... | collective-permute-start | bytes 786440 | tf_op jit(solution)/shard_map/while/body/eval_jaxpr/ppermute | solution.py:9
  365.5 11.6 %collective-permute-start = (f32[16,4096]{1,0:T(8,128)S(1)}, f32[16,4096]{1,0:T(8,128)S(1)}, u32[]{:S(2)}, u32[]{:S(2)}) collective-permute-start(f32[16,4096]{1,0:T(8,128)S(1)} %get-tuple-element.201), channel_id=1, source_target_pairs={{0,16},{16,32},{32,48},{48,64},{64,80},{80,96},{96,112},{112,128},... | collective-permute-start | bytes 786440 | tf_op jit(solution)/shard_map/while/body/eval_jaxpr/ppermute | solution.py:9
  377.6 11.6 %collective-permute-start = (f32[16,4096]{1,0:T(8,128)S(1)}, f32[16,4096]{1,0:T(8,128)S(1)}, u32[]{:S(2)}, u32[]{:S(2)}) collective-permute-start(f32[16,4096]{1,0:T(8,128)S(1)} %get-tuple-element.201), channel_id=1, source_target_pairs={{0,16},{16,32},{32,48},{48,64},{64,80},{80,96},{96,112},{112,128},... | collective-permute-start | bytes 786440 | tf_op jit(solution)/shard_map/while/body/eval_jaxpr/ppermute | solution.py:9
  389.7 11.6 %collective-permute-start = (f32[16,4096]{1,0:T(8,128)S(1)}, f32[16,4096]{1,0:T(8,128)S(1)}, u32[]{:S(2)}, u32[]{:S(2)}) collective-permute-start(f32[16,4096]{1,0:T(8,128)S(1)} %get-tuple-element.201), channel_id=1, source_target_pairs={{0,16},{16,32},{32,48},{48,64},{64,80},{80,96},{96,112},{112,128},... | collective-permute-start | bytes 786440 | tf_op jit(solution)/shard_map/while/body/eval_jaxpr/ppermute | solution.py:9
  401.7 11.6 %collective-permute-start = (f32[16,4096]{1,0:T(8,128)S(1)}, f32[16,4096]{1,0:T(8,128)S(1)}, u32[]{:S(2)}, u32[]{:S(2)}) collective-permute-start(f32[16,4096]{1,0:T(8,128)S(1)} %get-tuple-element.201), channel_id=1, source_target_pairs={{0,16},{16,32},{32,48},{48,64},{64,80},{80,96},{96,112},{112,128},... | collective-permute-start | bytes 786440 | tf_op jit(solution)/shard_map/while/body/eval_jaxpr/ppermute | solution.py:9
  413.8 11.6 %collective-permute-start = (f32[16,4096]{1,0:T(8,128)S(1)}, f32[16,4096]{1,0:T(8,128)S(1)}, u32[]{:S(2)}, u32[]{:S(2)}) collective-permute-start(f32[16,4096]{1,0:T(8,128)S(1)} %get-tuple-element.201), channel_id=1, source_target_pairs={{0,16},{16,32},{32,48},{48,64},{64,80},{80,96},{96,112},{112,128},... | collective-permute-start | bytes 786440 | tf_op jit(solution)/shard_map/while/body/eval_jaxpr/ppermute | solution.py:9
  425.9 11.6 %collective-permute-start = (f32[16,4096]{1,0:T(8,128)S(1)}, f32[16,4096]{1,0:T(8,128)S(1)}, u32[]{:S(2)}, u32[]{:S(2)}) collective-permute-start(f32[16,4096]{1,0:T(8,128)S(1)} %get-tuple-element.201), channel_id=1, source_target_pairs={{0,16},{16,32},{32,48},{48,64},{64,80},{80,96},{96,112},{112,128},... | collective-permute-start | bytes 786440 | tf_op jit(solution)/shard_map/while/body/eval_jaxpr/ppermute | solution.py:9
  438.0 11.6 %collective-permute-start = (f32[16,4096]{1,0:T(8,128)S(1)}, f32[16,4096]{1,0:T(8,128)S(1)}, u32[]{:S(2)}, u32[]{:S(2)}) collective-permute-start(f32[16,4096]{1,0:T(8,128)S(1)} %get-tuple-element.201), channel_id=1, source_target_pairs={{0,16},{16,32},{32,48},{48,64},{64,80},{80,96},{96,112},{112,128},... | collective-permute-start | bytes 786440 | tf_op jit(solution)/shard_map/while/body/eval_jaxpr/ppermute | solution.py:9
  450.0 11.6 %collective-permute-start = (f32[16,4096]{1,0:T(8,128)S(1)}, f32[16,4096]{1,0:T(8,128)S(1)}, u32[]{:S(2)}, u32[]{:S(2)}) collective-permute-start(f32[16,4096]{1,0:T(8,128)S(1)} %get-tuple-element.201), channel_id=1, source_target_pairs={{0,16},{16,32},{32,48},{48,64},{64,80},{80,96},{96,112},{112,128},... | collective-permute-start | bytes 786440 | tf_op jit(solution)/shard_map/while/body/eval_jaxpr/ppermute | solution.py:9
  462.1 11.6 %collective-permute-start = (f32[16,4096]{1,0:T(8,128)S(1)}, f32[16,4096]{1,0:T(8,128)S(1)}, u32[]{:S(2)}, u32[]{:S(2)}) collective-permute-start(f32[16,4096]{1,0:T(8,128)S(1)} %get-tuple-element.201), channel_id=1, source_target_pairs={{0,16},{16,32},{32,48},{48,64},{64,80},{80,96},{96,112},{112,128},... | collective-permute-start | bytes 786440 | tf_op jit(solution)/shard_map/while/body/eval_jaxpr/ppermute | solution.py:9
  474.2 11.6 %collective-permute-start = (f32[16,4096]{1,0:T(8,128)S(1)}, f32[16,4096]{1,0:T(8,128)S(1)}, u32[]{:S(2)}, u32[]{:S(2)}) collective-permute-start(f32[16,4096]{1,0:T(8,128)S(1)} %get-tuple-element.201), channel_id=1, source_target_pairs={{0,16},{16,32},{32,48},{48,64},{64,80},{80,96},{96,112},{112,128},... | collective-permute-start | bytes 786440 | tf_op jit(solution)/shard_map/while/body/eval_jaxpr/ppermute | solution.py:9
  486.3 11.6 %collective-permute-start = (f32[16,4096]{1,0:T(8,128)S(1)}, f32[16,4096]{1,0:T(8,128)S(1)}, u32[]{:S(2)}, u32[]{:S(2)}) collective-permute-start(f32[16,4096]{1,0:T(8,128)S(1)} %get-tuple-element.201), channel_id=1, source_target_pairs={{0,16},{16,32},{32,48},{48,64},{64,80},{80,96},{96,112},{112,128},... | collective-permute-start | bytes 786440 | tf_op jit(solution)/shard_map/while/body/eval_jaxpr/ppermute | solution.py:9
Sparse Core Ops, SparseCore 0:
  10.2 80.6 all-gather.2
where the time goes:
time: 509 us; the launch traced here: 507 us
  waiting for transfers between devices  358 us (70%)
  starting transfers between devices  98.1 us (19%)
  matrix products  28.6 us (6%)
  between operations  14.1 us (3%)
    ppermute x31, waiting for transfers between devices, from_behind(): return lax.ppermute(x, axis, [(i, (i + by) % count) for i in range(count)])  303 us
    ppermute x31, starting transfers between devices, from_behind(): return lax.ppermute(x, axis, [(i, (i + by) % count) for i in range(count)])  59.4 us
    all_to_all x1, waiting for transfers between devices, body(): lax.all_to_all(packed, 'group', split_axis=0, concat_axis=0, tiled=True)  22.5 us
    all_gather x1, waiting for transfers between devices, body(): gathered = lax.all_gather(own_passages, 'blk', axis=0, tiled=True)  20 us
    all_to_all x1, starting transfers between devices, body(): lax.all_to_all(live_flags, 'group', split_axis=0, concat_axis=0, tiled=True)  18.2 us
    all_to_all x1, starting transfers between devices, body(): lax.all_to_all(slot_grads, 'group', split_axis=0, concat_axis=0, tiled=True)  15.7 us
    dot_general x32, matrix products, contrib(): jnp.einsum('qp,qd->pd', coef_cols, query_rows, preferred_element_type=jnp...  15.3 us
    all_to_all x1, waiting for transfers between devices, body(): lax.all_to_all(live_flags, 'group', split_axis=0, concat_axis=0, tiled=True)  12.1 us
  transfers between devices with their start and end apart: 35, of which 34 were waited for; matrix products, arithmetic and copies ran while one was open for 4% of the time, Pallas kernels for 0%

commit v1 on v0

--- a/solution.py
+++ b/solution.py
@@ -51,7 +51,9 @@
     target_hot = (targets[:, None] == jnp.arange(total_rows, dtype=jnp.int32)[None, :]).astype(
         jnp.float32
     )
-    gathered = lax.all_gather(own_passages, "blk", axis=0, tiled=True)
+    gathered = jnp.concatenate(
+        lax.all_to_all(jnp.stack([own_passages] * lax.axis_size("blk")), "blk", 0, 0), axis=0
+    )
     in_scores = score_multiplier * jnp.einsum(
         "qd,pd->qp", query_rows, gathered, preferred_element_type=jnp.float32
     )

time: 509 us -> 568 us (1.12)
  waiting for transfers between devices: 358 us -> 410 us
  blocking collectives: 0 us -> 21.3 us
  between operations: 14.1 us -> 0.75 us
    all_to_all x1, waiting for transfers between devices: 22.5 us -> 92.8 us  [body(): lax.all_to_all(jnp.stack([own_passages] * lax.axis_size('blk')), 'blk', 0...]
    all_to_all x0 -> x1, blocking collectives: none -> 21.3 us  [body(): lax.all_to_all(packed, 'group', split_axis=0, concat_axis=0, tiled=True)]
    all_gather x1 -> x0, waiting for transfers between devices: 20 us -> none  [body(): gathered = lax.all_gather(own_passages, 'blk', axis=0, tiled=True)]
    all_to_all x1, starting transfers between devices: 15.7 us -> 6.41 us  [body(): lax.all_to_all(slot_grads, 'group', split_axis=0, concat_axis=0, tiled=True)]
  transfers between devices with their start and end apart: 35 -> 34, of which waited for: 34 -> 33; matrix products, arithmetic and copies ran while one was open for 4% -> 3% of each run, Pallas kernels for 0% -> 0%
where the time goes in v1:
time: 568 us; the launch traced here: 566 us
  waiting for transfers between devices  410 us (72%)
  starting transfers between devices  92.6 us (16%)
  matrix products  30.3 us (5%)
  blocking collectives  21.3 us (4%)
    ppermute x31, waiting for transfers between devices, from_behind(): return lax.ppermute(x, axis, [(i, (i + by) % count) for i in range(count)])  305 us
    all_to_all x1, waiting for transfers between devices, body(): lax.all_to_all(jnp.stack([own_passages] * lax.axis_size('blk')), 'blk', 0...  92.8 us
    ppermute x31, starting transfers between devices, from_behind(): return lax.ppermute(x, axis, [(i, (i + by) % count) for i in range(count)])  59.4 us
    all_to_all x1, blocking collectives, body(): lax.all_to_all(packed, 'group', split_axis=0, concat_axis=0, tiled=True)  21.3 us
    all_to_all x1, starting transfers between devices, body(): lax.all_to_all(live_flags, 'group', split_axis=0, concat_axis=0, tiled=True)  18.2 us
    dot_general x32, matrix products, contrib(): jnp.einsum('qp,qd->pd', coef_cols, query_rows, preferred_element_type=jnp...  15.3 us
    all_to_all x1, waiting for transfers between devices, body(): lax.all_to_all(live_flags, 'group', split_axis=0, concat_axis=0, tiled=True)  12.8 us
  transfers between devices with their start and end apart: 34, of which 33 were waited for; matrix products, arithmetic and copies ran while one was open for 3% of the time, Pallas kernels for 0%

profile of v1, /device:TPU:8, one launch (start us, length us, event | category | flops | bytes accessed | tf_op | source)
XLA Modules:
  0.0 565.9 jit_solution(3636467826412425699)
XLA Ops:
  3.7 18.2 %all-to-all-start.1 = ((bf16[16,1,2]{2,1,0:T(2,128)(2,1)}), bf16[16,1,2]{2,1,0:T(2,128)(2,1)S(1)}, u32[]{:S(2)}, u32[]{:S(2)}) async-start(bf16[16,1,2]{2,1,0:T(2,128)(2,1)} %all_to_all.20), calls=%async_computation.1 | async-start | bytes 16384 | tf_op jit(solution)/shard_map/all_to_all | solution.py:41
  22.5 12.8 %all-to-all-done.1 = bf16[16,1,2]{2,1,0:T(2,128)(2,1)S(1)} async-done(((bf16[16,1,2]{2,1,0:T(2,128)(2,1)}), bf16[16,1,2]{2,1,0:T(2,128)(2,1)S(1)}, u32[]{:S(2)}, u32[]{:S(2)}) %all-to-all-start.1) | async-done | bytes 96 | tf_op jit(solution)/shard_map/all_to_all | solution.py:41
  35.3 21.3 %all_to_all.25 = bf16[16,2,4096]{2,1,0:T(2,128)(2,1)S(1)} all-to-all(bf16[16,2,4096]{2,1,0:T(2,128)(2,1)S(1)} %reshape.104), channel_id=1, replica_groups=mesh['blk'=32,'group'=16] {'group'}, dimensions={0} | all-to-all | bytes 524288 | tf_op jit(solution)/shard_map/all_to_all | solution.py:40
  56.6 3.4 stack.3
  59.9 8.6 %all-to-all-start = ((bf16[32,16,4096]{2,1,0:T(8,128)(2,1)}), bf16[32,16,4096]{2,1,0:T(8,128)(2,1)}, u32[]{:S(2)}, u32[]{:S(2)}) async-start(bf16[32,16,4096]{2,1,0:T(8,128)(2,1)} %stack.3), calls=%async_computation | async-start | bytes 8388608 | tf_op jit(solution)/shard_map/all_to_all | solution.py:55
  69.6 92.8 %all-to-all-done = bf16[32,16,4096]{2,1,0:T(8,128)(2,1)} async-done(((bf16[32,16,4096]{2,1,0:T(8,128)(2,1)}), bf16[32,16,4096]{2,1,0:T(8,128)(2,1)}, u32[]{:S(2)}, u32[]{:S(2)}) %all-to-all-start) | async-done | bytes 4194336 | tf_op jit(solution)/shard_map/all_to_all | solution.py:55
  162.5 3.6 fusion.31
  167.0 5.6 fusion.9
  173.2 3.3 fusion.4
  177.4 6.4 %all-to-all-start.3 = ((bf16[16,2,4096]{2,1,0:T(2,128)(2,1)}), bf16[16,2,4096]{2,1,0:T(2,128)(2,1)S(1)}, u32[]{:S(2)}, u32[]{:S(2)}) async-start(bf16[16,2,4096]{2,1,0:T(2,128)(2,1)} %reshape.106), calls=%async_computation.3 | async-start | bytes 524288 | tf_op jit(solution)/shard_map/all_to_all | solution.py:96
  184.3 379.9 %while.15 = (s32[]{:T(128)}, f32[16,4096]{1,0:T(8,128)S(1)}, s32[]{:T(128)}, bf16[256,512]{1,0:T(8,128)(2,1)S(1)}, bf16[256,4096]{1,0:T(8,128)(2,1)S(1)}, /*inde...) while((s32[]{:T(128)}, f32[16,4096]{1,0:T(8,128)S(1)}, ...), condition=%wide.region_9.10_spmd, body=%wide.region_8.9_spmd.sunk | while | flops 33619984 | bytes 3735892 | solution.py:86
  184.3 1.9 collective-permute-start
  186.3 15.2 %collective-permute-done = f32[16,4096]{1,0:T(8,128)S(1)} collective-permute-done((f32[16,4096]{1,0:T(8,128)S(1)}, f32[16,4096]{1,0:T(8,128)S(1)}, u32[]{:S(2)}, u32[]{:S(2)}) %collective-permute-start) | collective-permute-done | bytes 262176 | tf_op jit(solution)/shard_map/while/body/eval_jaxpr/ppermute | solution.py:9
  202.0 1.9 collective-permute-start
  203.9 9.6 %collective-permute-done = f32[16,4096]{1,0:T(8,128)S(1)} collective-permute-done((f32[16,4096]{1,0:T(8,128)S(1)}, f32[16,4096]{1,0:T(8,128)S(1)}, u32[]{:S(2)}, u32[]{:S(2)}) %collective-permute-start) | collective-permute-done | bytes 262176 | tf_op jit(solution)/shard_map/while/body/eval_jaxpr/ppermute | solution.py:9
  214.1 1.9 collective-permute-start
  216.0 9.6 %collective-permute-done = f32[16,4096]{1,0:T(8,128)S(1)} collective-permute-done((f32[16,4096]{1,0:T(8,128)S(1)}, f32[16,4096]{1,0:T(8,128)S(1)}, u32[]{:S(2)}, u32[]{:S(2)}) %collective-permute-start) | collective-permute-done | bytes 262176 | tf_op jit(solution)/shard_map/while/body/eval_jaxpr/ppermute | solution.py:9
  226.1 1.9 collective-permute-start
  228.1 9.6 %collective-permute-done = f32[16,4096]{1,0:T(8,128)S(1)} collective-permute-done((f32[16,4096]{1,0:T(8,128)S(1)}, f32[16,4096]{1,0:T(8,128)S(1)}, u32[]{:S(2)}, u32[]{:S(2)}) %collective-permute-start) | collective-permute-done | bytes 262176 | tf_op jit(solution)/shard_map/while/body/eval_jaxpr/ppermute | solution.py:9
  240.2 9.6 %collective-permute-done = f32[16,4096]{1,0:T(8,128)S(1)} collective-permute-done((f32[16,4096]{1,0:T(8,128)S(1)}, f32[16,4096]{1,0:T(8,128)S(1)}, u32[]{:S(2)}, u32[]{:S(2)}) %collective-permute-start) | collective-permute-done | bytes 262176 | tf_op jit(solution)/shard_map/while/body/eval_jaxpr/ppermute | solution.py:9
  252.2 9.6 %collective-permute-done = f32[16,4096]{1,0:T(8,128)S(1)} collective-permute-done((f32[16,4096]{1,0:T(8,128)S(1)}, f32[16,4096]{1,0:T(8,128)S(1)}, u32[]{:S(2)}, u32[]{:S(2)}) %collective-permute-start) | collective-permute-done | bytes 262176 | tf_op jit(solution)/shard_map/while/body/eval_jaxpr/ppermute | solution.py:9
  262.4 1.9 collective-permute-start
  264.3 9.6 %collective-permute-done = f32[16,4096]{1,0:T(8,128)S(1)} collective-permute-done((f32[16,4096]{1,0:T(8,128)S(1)}, f32[16,4096]{1,0:T(8,128)S(1)}, u32[]{:S(2)}, u32[]{:S(2)}) %collective-permute-start) | collective-permute-done | bytes 262176 | tf_op jit(solution)/shard_map/while/body/eval_jaxpr/ppermute | solution.py:9
  274.4 1.9 collective-permute-start
  276.4 9.6 %collective-permute-done = f32[16,4096]{1,0:T(8,128)S(1)} collective-permute-done((f32[16,4096]{1,0:T(8,128)S(1)}, f32[16,4096]{1,0:T(8,128)S(1)}, u32[]{:S(2)}, u32[]{:S(2)}) %collective-permute-start) | collective-permute-done | bytes 262176 | tf_op jit(solution)/shard_map/while/body/eval_jaxpr/ppermute | solution.py:9
  288.5 9.6 %collective-permute-done = f32[16,4096]{1,0:T(8,128)S(1)} collective-permute-done((f32[16,4096]{1,0:T(8,128)S(1)}, f32[16,4096]{1,0:T(8,128)S(1)}, u32[]{:S(2)}, u32[]{:S(2)}) %collective-permute-start) | collective-permute-done | bytes 262176 | tf_op jit(solution)/shard_map/while/body/eval_jaxpr/ppermute | solution.py:9
  300.5 9.6 %collective-permute-done = f32[16,4096]{1,0:T(8,128)S(1)} collective-permute-done((f32[16,4096]{1,0:T(8,128)S(1)}, f32[16,4096]{1,0:T(8,128)S(1)}, u32[]{:S(2)}, u32[]{:S(2)}) %collective-permute-start) | collective-permute-done | bytes 262176 | tf_op jit(solution)/shard_map/while/body/eval_jaxpr/ppermute | solution.py:9
  312.6 9.6 %collective-permute-done = f32[16,4096]{1,0:T(8,128)S(1)} collective-permute-done((f32[16,4096]{1,0:T(8,128)S(1)}, f32[16,4096]{1,0:T(8,128)S(1)}, u32[]{:S(2)}, u32[]{:S(2)}) %collective-permute-start) | collective-permute-done | bytes 262176 | tf_op jit(solution)/shard_map/while/body/eval_jaxpr/ppermute | solution.py:9
  324.7 9.6 %collective-permute-done = f32[16,4096]{1,0:T(8,128)S(1)} collective-permute-done((f32[16,4096]{1,0:T(8,128)S(1)}, f32[16,4096]{1,0:T(8,128)S(1)}, u32[]{:S(2)}, u32[]{:S(2)}) %collective-permute-start) | collective-permute-done | bytes 262176 | tf_op jit(solution)/shard_map/while/body/eval_jaxpr/ppermute | solution.py:9
  336.8 9.6 %collective-permute-done = f32[16,4096]{1,0:T(8,128)S(1)} collective-permute-done((f32[16,4096]{1,0:T(8,128)S(1)}, f32[16,4096]{1,0:T(8,128)S(1)}, u32[]{:S(2)}, u32[]{:S(2)}) %collective-permute-start) | collective-permute-done | bytes 262176 | tf_op jit(solution)/shard_map/while/body/eval_jaxpr/ppermute | solution.py:9
  348.8 9.6 %collective-permute-done = f32[16,4096]{1,0:T(8,128)S(1)} collective-permute-done((f32[16,4096]{1,0:T(8,128)S(1)}, f32[16,4096]{1,0:T(8,128)S(1)}, u32[]{:S(2)}, u32[]{:S(2)}) %collective-permute-start) | collective-permute-done | bytes 262176 | tf_op jit(solution)/shard_map/while/body/eval_jaxpr/ppermute | solution.py:9
  360.9 9.6 %collective-permute-done = f32[16,4096]{1,0:T(8,128)S(1)} collective-permute-done((f32[16,4096]{1,0:T(8,128)S(1)}, f32[16,4096]{1,0:T(8,128)S(1)}, u32[]{:S(2)}, u32[]{:S(2)}) %collective-permute-start) | collective-permute-done | bytes 262176 | tf_op jit(solution)/shard_map/while/body/eval_jaxpr/ppermute | solution.py:9
  373.0 9.6 %collective-permute-done = f32[16,4096]{1,0:T(8,128)S(1)} collective-permute-done((f32[16,4096]{1,0:T(8,128)S(1)}, f32[16,4096]{1,0:T(8,128)S(1)}, u32[]{:S(2)}, u32[]{:S(2)}) %collective-permute-start) | collective-permute-done | bytes 262176 | tf_op jit(solution)/shard_map/while/body/eval_jaxpr/ppermute | solution.py:9
  385.1 9.6 %collective-permute-done = f32[16,4096]{1,0:T(8,128)S(1)} collective-permute-done((f32[16,4096]{1,0:T(8,128)S(1)}, f32[16,4096]{1,0:T(8,128)S(1)}, u32[]{:S(2)}, u32[]{:S(2)}) %collective-permute-start) | collective-permute-done | bytes 262176 | tf_op jit(solution)/shard_map/while/body/eval_jaxpr/ppermute | solution.py:9
  397.1 9.6 %collective-permute-done = f32[16,4096]{1,0:T(8,128)S(1)} collective-permute-done((f32[16,4096]{1,0:T(8,128)S(1)}, f32[16,4096]{1,0:T(8,128)S(1)}, u32[]{:S(2)}, u32[]{:S(2)}) %collective-permute-start) | collective-permute-done | bytes 262176 | tf_op jit(solution)/shard_map/while/body/eval_jaxpr/ppermute | solution.py:9
  409.2 9.6 %collective-permute-done = f32[16,4096]{1,0:T(8,128)S(1)} collective-permute-done((f32[16,4096]{1,0:T(8,128)S(1)}, f32[16,4096]{1,0:T(8,128)S(1)}, u32[]{:S(2)}, u32[]{:S(2)}) %collective-permute-start) | collective-permute-done | bytes 262176 | tf_op jit(solution)/shard_map/while/body/eval_jaxpr/ppermute | solution.py:9
  421.3 9.6 %collective-permute-done = f32[16,4096]{1,0:T(8,128)S(1)} collective-permute-done((f32[16,4096]{1,0:T(8,128)S(1)}, f32[16,4096]{1,0:T(8,128)S(1)}, u32[]{:S(2)}, u32[]{:S(2)}) %collective-permute-start) | collective-permute-done | bytes 262176 | tf_op jit(solution)/shard_map/while/body/eval_jaxpr/ppermute | solution.py:9
  433.4 9.6 %collective-permute-done = f32[16,4096]{1,0:T(8,128)S(1)} collective-permute-done((f32[16,4096]{1,0:T(8,128)S(1)}, f32[16,4096]{1,0:T(8,128)S(1)}, u32[]{:S(2)}, u32[]{:S(2)}) %collective-permute-start) | collective-permute-done | bytes 262176 | tf_op jit(solution)/shard_map/while/body/eval_jaxpr/ppermute | solution.py:9
  445.4 9.6 %collective-permute-done = f32[16,4096]{1,0:T(8,128)S(1)} collective-permute-done((f32[16,4096]{1,0:T(8,128)S(1)}, f32[16,4096]{1,0:T(8,128)S(1)}, u32[]{:S(2)}, u32[]{:S(2)}) %collective-permute-start) | collective-permute-done | bytes 262176 | tf_op jit(solution)/shard_map/while/body/eval_jaxpr/ppermute | solution.py:9
  457.5 9.6 %collective-permute-done = f32[16,4096]{1,0:T(8,128)S(1)} collective-permute-done((f32[16,4096]{1,0:T(8,128)S(1)}, f32[16,4096]{1,0:T(8,128)S(1)}, u32[]{:S(2)}, u32[]{:S(2)}) %collective-permute-start) | collective-permute-done | bytes 262176 | tf_op jit(solution)/shard_map/while/body/eval_jaxpr/ppermute | solution.py:9
  469.6 9.6 %collective-permute-done = f32[16,4096]{1,0:T(8,128)S(1)} collective-permute-done((f32[16,4096]{1,0:T(8,128)S(1)}, f32[16,4096]{1,0:T(8,128)S(1)}, u32[]{:S(2)}, u32[]{:S(2)}) %collective-permute-start) | collective-permute-done | bytes 262176 | tf_op jit(solution)/shard_map/while/body/eval_jaxpr/ppermute | solution.py:9
  481.7 9.6 %collective-permute-done = f32[16,4096]{1,0:T(8,128)S(1)} collective-permute-done((f32[16,4096]{1,0:T(8,128)S(1)}, f32[16,4096]{1,0:T(8,128)S(1)}, u32[]{:S(2)}, u32[]{:S(2)}) %collective-permute-start) | collective-permute-done | bytes 262176 | tf_op jit(solution)/shard_map/while/body/eval_jaxpr/ppermute | solution.py:9
  493.7 9.6 %collective-permute-done = f32[16,4096]{1,0:T(8,128)S(1)} collective-permute-done((f32[16,4096]{1,0:T(8,128)S(1)}, f32[16,4096]{1,0:T(8,128)S(1)}, u32[]{:S(2)}, u32[]{:S(2)}) %collective-permute-start) | collective-permute-done | bytes 262176 | tf_op jit(solution)/shard_map/while/body/eval_jaxpr/ppermute | solution.py:9
  505.8 9.6 %collective-permute-done = f32[16,4096]{1,0:T(8,128)S(1)} collective-permute-done((f32[16,4096]{1,0:T(8,128)S(1)}, f32[16,4096]{1,0:T(8,128)S(1)}, u32[]{:S(2)}, u32[]{:S(2)}) %collective-permute-start) | collective-permute-done | bytes 262176 | tf_op jit(solution)/shard_map/while/body/eval_jaxpr/ppermute | solution.py:9
  517.9 9.6 %collective-permute-done = f32[16,4096]{1,0:T(8,128)S(1)} collective-permute-done((f32[16,4096]{1,0:T(8,128)S(1)}, f32[16,4096]{1,0:T(8,128)S(1)}, u32[]{:S(2)}, u32[]{:S(2)}) %collective-permute-start) | collective-permute-done | bytes 262176 | tf_op jit(solution)/shard_map/while/body/eval_jaxpr/ppermute | solution.py:9
  530.0 9.6 %collective-permute-done = f32[16,4096]{1,0:T(8,128)S(1)} collective-permute-done((f32[16,4096]{1,0:T(8,128)S(1)}, f32[16,4096]{1,0:T(8,128)S(1)}, u32[]{:S(2)}, u32[]{:S(2)}) %collective-permute-start) | collective-permute-done | bytes 262176 | tf_op jit(solution)/shard_map/while/body/eval_jaxpr/ppermute | solution.py:9
  542.0 9.6 %collective-permute-done = f32[16,4096]{1,0:T(8,128)S(1)} collective-permute-done((f32[16,4096]{1,0:T(8,128)S(1)}, f32[16,4096]{1,0:T(8,128)S(1)}, u32[]{:S(2)}, u32[]{:S(2)}) %collective-permute-start) | collective-permute-done | bytes 262176 | tf_op jit(solution)/shard_map/while/body/eval_jaxpr/ppermute | solution.py:9
  554.1 9.6 %collective-permute-done = f32[16,4096]{1,0:T(8,128)S(1)} collective-permute-done((f32[16,4096]{1,0:T(8,128)S(1)}, f32[16,4096]{1,0:T(8,128)S(1)}, u32[]{:S(2)}, u32[]{:S(2)}) %collective-permute-start) | collective-permute-done | bytes 262176 | tf_op jit(solution)/shard_map/while/body/eval_jaxpr/ppermute | solution.py:9
  (86 shorter events, 72.0 us)
Async XLA Ops:
  0.6 21.3 %copy-start = (bf16[1,16,4096]{2,1,0:T(8,128)(2,1)S(1)}, bf16[1,16,4096]{2,1,0:T(8,128)(2,1)}, u32[]{:S(2)}) copy-start(bf16[1,16,4096]{2,1,0:T(8,128)(2,1)} %param.10) | copy-start | bytes 393220
  3.7 31.5 %all-to-all-start.1 = ((bf16[16,1,2]{2,1,0:T(2,128)(2,1)}), bf16[16,1,2]{2,1,0:T(2,128)(2,1)S(1)}, u32[]{:S(2)}, u32[]{:S(2)}) async-start(bf16[16,1,2]{2,1,0:T(2,128)(2,1)} %all_to_all.20), calls=%async_computation.1 | async-start | bytes 16384 | tf_op jit(solution)/shard_map/all_to_all | solution.py:41
  59.9 8.9 %copy-start.1 = (bf16[1,256,4096]{2,1,0:T(8,128)(2,1)S(1)}, bf16[1,256,4096]{2,1,0:T(8,128)(2,1)}, u32[]{:S(2)}) copy-start(bf16[1,256,4096]{2,1,0:T(8,128)(2,1)} %param.7) | copy-start | bytes 6291460
  59.9 102.5 %all-to-all-start = ((bf16[32,16,4096]{2,1,0:T(8,128)(2,1)}), bf16[32,16,4096]{2,1,0:T(8,128)(2,1)}, u32[]{:S(2)}, u32[]{:S(2)}) async-start(bf16[32,16,4096]{2,1,0:T(8,128)(2,1)} %stack.3), calls=%async_computation | async-start | bytes 8388608 | tf_op jit(solution)/shard_map/all_to_all | solution.py:55
  162.5 3.6 copy-start.2
  177.4 387.5 %all-to-all-start.3 = ((bf16[16,2,4096]{2,1,0:T(2,128)(2,1)}), bf16[16,2,4096]{2,1,0:T(2,128)(2,1)S(1)}, u32[]{:S(2)}, u32[]{:S(2)}) async-start(bf16[16,2,4096]{2,1,0:T(2,128)(2,1)} %reshape.106), calls=%async_computation.3 | async-start | bytes 524288 | tf_op jit(solution)/shard_map/all_to_all | solution.py:96
  184.3 17.2 %collective-permute-start = (f32[16,4096]{1,0:T(8,128)S(1)}, f32[16,4096]{1,0:T(8,128)S(1)}, u32[]{:S(2)}, u32[]{:S(2)}) collective-permute-start(f32[16,4096]{1,0:T(8,128)S(1)} %get-tuple-element.201), channel_id=1, source_target_pairs={{0,16},{16,32},{32,48},{48,64},{64,80},{80,96},{96,112},{112,128},... | collective-permute-start | bytes 786440 | tf_op jit(solution)/shard_map/while/body/eval_jaxpr/ppermute | solution.py:9
  202.0 11.6 %collective-permute-start = (f32[16,4096]{1,0:T(8,128)S(1)}, f32[16,4096]{1,0:T(8,128)S(1)}, u32[]{:S(2)}, u32[]{:S(2)}) collective-permute-start(f32[16,4096]{1,0:T(8,128)S(1)} %get-tuple-element.201), channel_id=1, source_target_pairs={{0,16},{16,32},{32,48},{48,64},{64,80},{80,96},{96,112},{112,128},... | collective-permute-start | bytes 786440 | tf_op jit(solution)/shard_map/while/body/eval_jaxpr/ppermute | solution.py:9
  214.1 11.6 %collective-permute-start = (f32[16,4096]{1,0:T(8,128)S(1)}, f32[16,4096]{1,0:T(8,128)S(1)}, u32[]{:S(2)}, u32[]{:S(2)}) collective-permute-start(f32[16,4096]{1,0:T(8,128)S(1)} %get-tuple-element.201), channel_id=1, source_target_pairs={{0,16},{16,32},{32,48},{48,64},{64,80},{80,96},{96,112},{112,128},... | collective-permute-start | bytes 786440 | tf_op jit(solution)/shard_map/while/body/eval_jaxpr/ppermute | solution.py:9
  226.1 11.6 %collective-permute-start = (f32[16,4096]{1,0:T(8,128)S(1)}, f32[16,4096]{1,0:T(8,128)S(1)}, u32[]{:S(2)}, u32[]{:S(2)}) collective-permute-start(f32[16,4096]{1,0:T(8,128)S(1)} %get-tuple-element.201), channel_id=1, source_target_pairs={{0,16},{16,32},{32,48},{48,64},{64,80},{80,96},{96,112},{112,128},... | collective-permute-start | bytes 786440 | tf_op jit(solution)/shard_map/while/body/eval_jaxpr/ppermute | solution.py:9
  238.2 11.6 %collective-permute-start = (f32[16,4096]{1,0:T(8,128)S(1)}, f32[16,4096]{1,0:T(8,128)S(1)}, u32[]{:S(2)}, u32[]{:S(2)}) collective-permute-start(f32[16,4096]{1,0:T(8,128)S(1)} %get-tuple-element.201), channel_id=1, source_target_pairs={{0,16},{16,32},{32,48},{48,64},{64,80},{80,96},{96,112},{112,128},... | collective-permute-start | bytes 786440 | tf_op jit(solution)/shard_map/while/body/eval_jaxpr/ppermute | solution.py:9
  250.3 11.6 %collective-permute-start = (f32[16,4096]{1,0:T(8,128)S(1)}, f32[16,4096]{1,0:T(8,128)S(1)}, u32[]{:S(2)}, u32[]{:S(2)}) collective-permute-start(f32[16,4096]{1,0:T(8,128)S(1)} %get-tuple-element.201), channel_id=1, source_target_pairs={{0,16},{16,32},{32,48},{48,64},{64,80},{80,96},{96,112},{112,128},... | collective-permute-start | bytes 786440 | tf_op jit(solution)/shard_map/while/body/eval_jaxpr/ppermute | solution.py:9
  262.4 11.6 %collective-permute-start = (f32[16,4096]{1,0:T(8,128)S(1)}, f32[16,4096]{1,0:T(8,128)S(1)}, u32[]{:S(2)}, u32[]{:S(2)}) collective-permute-start(f32[16,4096]{1,0:T(8,128)S(1)} %get-tuple-element.201), channel_id=1, source_target_pairs={{0,16},{16,32},{32,48},{48,64},{64,80},{80,96},{96,112},{112,128},... | collective-permute-start | bytes 786440 | tf_op jit(solution)/shard_map/while/body/eval_jaxpr/ppermute | solution.py:9
  274.4 11.6 %collective-permute-start = (f32[16,4096]{1,0:T(8,128)S(1)}, f32[16,4096]{1,0:T(8,128)S(1)}, u32[]{:S(2)}, u32[]{:S(2)}) collective-permute-start(f32[16,4096]{1,0:T(8,128)S(1)} %get-tuple-element.201), channel_id=1, source_target_pairs={{0,16},{16,32},{32,48},{48,64},{64,80},{80,96},{96,112},{112,128},... | collective-permute-start | bytes 786440 | tf_op jit(solution)/shard_map/while/body/eval_jaxpr/ppermute | solution.py:9
  286.5 11.6 %collective-permute-start = (f32[16,4096]{1,0:T(8,128)S(1)}, f32[16,4096]{1,0:T(8,128)S(1)}, u32[]{:S(2)}, u32[]{:S(2)}) collective-permute-start(f32[16,4096]{1,0:T(8,128)S(1)} %get-tuple-element.201), channel_id=1, source_target_pairs={{0,16},{16,32},{32,48},{48,64},{64,80},{80,96},{96,112},{112,128},... | collective-permute-start | bytes 786440 | tf_op jit(solution)/shard_map/while/body/eval_jaxpr/ppermute | solution.py:9
  298.6 11.6 %collective-permute-start = (f32[16,4096]{1,0:T(8,128)S(1)}, f32[16,4096]{1,0:T(8,128)S(1)}, u32[]{:S(2)}, u32[]{:S(2)}) collective-permute-start(f32[16,4096]{1,0:T(8,128)S(1)} %get-tuple-element.201), channel_id=1, source_target_pairs={{0,16},{16,32},{32,48},{48,64},{64,80},{80,96},{96,112},{112,128},... | collective-permute-start | bytes 786440 | tf_op jit(solution)/shard_map/while/body/eval_jaxpr/ppermute | solution.py:9
  310.7 11.6 %collective-permute-start = (f32[16,4096]{1,0:T(8,128)S(1)}, f32[16,4096]{1,0:T(8,128)S(1)}, u32[]{:S(2)}, u32[]{:S(2)}) collective-permute-start(f32[16,4096]{1,0:T(8,128)S(1)} %get-tuple-element.201), channel_id=1, source_target_pairs={{0,16},{16,32},{32,48},{48,64},{64,80},{80,96},{96,112},{112,128},... | collective-permute-start | bytes 786440 | tf_op jit(solution)/shard_map/while/body/eval_jaxpr/ppermute | solution.py:9
  322.7 11.6 %collective-permute-start = (f32[16,4096]{1,0:T(8,128)S(1)}, f32[16,4096]{1,0:T(8,128)S(1)}, u32[]{:S(2)}, u32[]{:S(2)}) collective-permute-start(f32[16,4096]{1,0:T(8,128)S(1)} %get-tuple-element.201), channel_id=1, source_target_pairs={{0,16},{16,32},{32,48},{48,64},{64,80},{80,96},{96,112},{112,128},... | collective-permute-start | bytes 786440 | tf_op jit(solution)/shard_map/while/body/eval_jaxpr/ppermute | solution.py:9
  334.8 11.6 %collective-permute-start = (f32[16,4096]{1,0:T(8,128)S(1)}, f32[16,4096]{1,0:T(8,128)S(1)}, u32[]{:S(2)}, u32[]{:S(2)}) collective-permute-start(f32[16,4096]{1,0:T(8,128)S(1)} %get-tuple-element.201), channel_id=1, source_target_pairs={{0,16},{16,32},{32,48},{48,64},{64,80},{80,96},{96,112},{112,128},... | collective-permute-start | bytes 786440 | tf_op jit(solution)/shard_map/while/body/eval_jaxpr/ppermute | solution.py:9
  346.9 11.6 %collective-permute-start = (f32[16,4096]{1,0:T(8,128)S(1)}, f32[16,4096]{1,0:T(8,128)S(1)}, u32[]{:S(2)}, u32[]{:S(2)}) collective-permute-start(f32[16,4096]{1,0:T(8,128)S(1)} %get-tuple-element.201), channel_id=1, source_target_pairs={{0,16},{16,32},{32,48},{48,64},{64,80},{80,96},{96,112},{112,128},... | collective-permute-start | bytes 786440 | tf_op jit(solution)/shard_map/while/body/eval_jaxpr/ppermute | solution.py:9
  359.0 11.6 %collective-permute-start = (f32[16,4096]{1,0:T(8,128)S(1)}, f32[16,4096]{1,0:T(8,128)S(1)}, u32[]{:S(2)}, u32[]{:S(2)}) collective-permute-start(f32[16,4096]{1,0:T(8,128)S(1)} %get-tuple-element.201), channel_id=1, source_target_pairs={{0,16},{16,32},{32,48},{48,64},{64,80},{80,96},{96,112},{112,128},... | collective-permute-start | bytes 786440 | tf_op jit(solution)/shard_map/while/body/eval_jaxpr/ppermute | solution.py:9
  371.0 11.6 %collective-permute-start = (f32[16,4096]{1,0:T(8,128)S(1)}, f32[16,4096]{1,0:T(8,128)S(1)}, u32[]{:S(2)}, u32[]{:S(2)}) collective-permute-start(f32[16,4096]{1,0:T(8,128)S(1)} %get-tuple-element.201), channel_id=1, source_target_pairs={{0,16},{16,32},{32,48},{48,64},{64,80},{80,96},{96,112},{112,128},... | collective-permute-start | bytes 786440 | tf_op jit(solution)/shard_map/while/body/eval_jaxpr/ppermute | solution.py:9
  383.1 11.6 %collective-permute-start = (f32[16,4096]{1,0:T(8,128)S(1)}, f32[16,4096]{1,0:T(8,128)S(1)}, u32[]{:S(2)}, u32[]{:S(2)}) collective-permute-start(f32[16,4096]{1,0:T(8,128)S(1)} %get-tuple-element.201), channel_id=1, source_target_pairs={{0,16},{16,32},{32,48},{48,64},{64,80},{80,96},{96,112},{112,128},... | collective-permute-start | bytes 786440 | tf_op jit(solution)/shard_map/while/body/eval_jaxpr/ppermute | solution.py:9
  395.2 11.6 %collective-permute-start = (f32[16,4096]{1,0:T(8,128)S(1)}, f32[16,4096]{1,0:T(8,128)S(1)}, u32[]{:S(2)}, u32[]{:S(2)}) collective-permute-start(f32[16,4096]{1,0:T(8,128)S(1)} %get-tuple-element.201), channel_id=1, source_target_pairs={{0,16},{16,32},{32,48},{48,64},{64,80},{80,96},{96,112},{112,128},... | collective-permute-start | bytes 786440 | tf_op jit(solution)/shard_map/while/body/eval_jaxpr/ppermute | solution.py:9
  407.3 11.6 %collective-permute-start = (f32[16,4096]{1,0:T(8,128)S(1)}, f32[16,4096]{1,0:T(8,128)S(1)}, u32[]{:S(2)}, u32[]{:S(2)}) collective-permute-start(f32[16,4096]{1,0:T(8,128)S(1)} %get-tuple-element.201), channel_id=1, source_target_pairs={{0,16},{16,32},{32,48},{48,64},{64,80},{80,96},{96,112},{112,128},... | collective-permute-start | bytes 786440 | tf_op jit(solution)/shard_map/while/body/eval_jaxpr/ppermute | solution.py:9
  419.3 11.6 %collective-permute-start = (f32[16,4096]{1,0:T(8,128)S(1)}, f32[16,4096]{1,0:T(8,128)S(1)}, u32[]{:S(2)}, u32[]{:S(2)}) collective-permute-start(f32[16,4096]{1,0:T(8,128)S(1)} %get-tuple-element.201), channel_id=1, source_target_pairs={{0,16},{16,32},{32,48},{48,64},{64,80},{80,96},{96,112},{112,128},... | collective-permute-start | bytes 786440 | tf_op jit(solution)/shard_map/while/body/eval_jaxpr/ppermute | solution.py:9
  431.4 11.6 %collective-permute-start = (f32[16,4096]{1,0:T(8,128)S(1)}, f32[16,4096]{1,0:T(8,128)S(1)}, u32[]{:S(2)}, u32[]{:S(2)}) collective-permute-start(f32[16,4096]{1,0:T(8,128)S(1)} %get-tuple-element.201), channel_id=1, source_target_pairs={{0,16},{16,32},{32,48},{48,64},{64,80},{80,96},{96,112},{112,128},... | collective-permute-start | bytes 786440 | tf_op jit(solution)/shard_map/while/body/eval_jaxpr/ppermute | solution.py:9
  443.5 11.6 %collective-permute-start = (f32[16,4096]{1,0:T(8,128)S(1)}, f32[16,4096]{1,0:T(8,128)S(1)}, u32[]{:S(2)}, u32[]{:S(2)}) collective-permute-start(f32[16,4096]{1,0:T(8,128)S(1)} %get-tuple-element.201), channel_id=1, source_target_pairs={{0,16},{16,32},{32,48},{48,64},{64,80},{80,96},{96,112},{112,128},... | collective-permute-start | bytes 786440 | tf_op jit(solution)/shard_map/while/body/eval_jaxpr/ppermute | solution.py:9
  455.6 11.6 %collective-permute-start = (f32[16,4096]{1,0:T(8,128)S(1)}, f32[16,4096]{1,0:T(8,128)S(1)}, u32[]{:S(2)}, u32[]{:S(2)}) collective-permute-start(f32[16,4096]{1,0:T(8,128)S(1)} %get-tuple-element.201), channel_id=1, source_target_pairs={{0,16},{16,32},{32,48},{48,64},{64,80},{80,96},{96,112},{112,128},... | collective-permute-start | bytes 786440 | tf_op jit(solution)/shard_map/while/body/eval_jaxpr/ppermute | solution.py:9
  467.6 11.6 %collective-permute-start = (f32[16,4096]{1,0:T(8,128)S(1)}, f32[16,4096]{1,0:T(8,128)S(1)}, u32[]{:S(2)}, u32[]{:S(2)}) collective-permute-start(f32[16,4096]{1,0:T(8,128)S(1)} %get-tuple-element.201), channel_id=1, source_target_pairs={{0,16},{16,32},{32,48},{48,64},{64,80},{80,96},{96,112},{112,128},... | collective-permute-start | bytes 786440 | tf_op jit(solution)/shard_map/while/body/eval_jaxpr/ppermute | solution.py:9
  479.7 11.6 %collective-permute-start = (f32[16,4096]{1,0:T(8,128)S(1)}, f32[16,4096]{1,0:T(8,128)S(1)}, u32[]{:S(2)}, u32[]{:S(2)}) collective-permute-start(f32[16,4096]{1,0:T(8,128)S(1)} %get-tuple-element.201), channel_id=1, source_target_pairs={{0,16},{16,32},{32,48},{48,64},{64,80},{80,96},{96,112},{112,128},... | collective-permute-start | bytes 786440 | tf_op jit(solution)/shard_map/while/body/eval_jaxpr/ppermute | solution.py:9
  491.8 11.6 %collective-permute-start = (f32[16,4096]{1,0:T(8,128)S(1)}, f32[16,4096]{1,0:T(8,128)S(1)}, u32[]{:S(2)}, u32[]{:S(2)}) collective-permute-start(f32[16,4096]{1,0:T(8,128)S(1)} %get-tuple-element.201), channel_id=1, source_target_pairs={{0,16},{16,32},{32,48},{48,64},{64,80},{80,96},{96,112},{112,128},... | collective-permute-start | bytes 786440 | tf_op jit(solution)/shard_map/while/body/eval_jaxpr/ppermute | solution.py:9
  503.9 11.6 %collective-permute-start = (f32[16,4096]{1,0:T(8,128)S(1)}, f32[16,4096]{1,0:T(8,128)S(1)}, u32[]{:S(2)}, u32[]{:S(2)}) collective-permute-start(f32[16,4096]{1,0:T(8,128)S(1)} %get-tuple-element.201), channel_id=1, source_target_pairs={{0,16},{16,32},{32,48},{48,64},{64,80},{80,96},{96,112},{112,128},... | collective-permute-start | bytes 786440 | tf_op jit(solution)/shard_map/while/body/eval_jaxpr/ppermute | solution.py:9
  515.9 11.6 %collective-permute-start = (f32[16,4096]{1,0:T(8,128)S(1)}, f32[16,4096]{1,0:T(8,128)S(1)}, u32[]{:S(2)}, u32[]{:S(2)}) collective-permute-start(f32[16,4096]{1,0:T(8,128)S(1)} %get-tuple-element.201), channel_id=1, source_target_pairs={{0,16},{16,32},{32,48},{48,64},{64,80},{80,96},{96,112},{112,128},... | collective-permute-start | bytes 786440 | tf_op jit(solution)/shard_map/while/body/eval_jaxpr/ppermute | solution.py:9
  528.0 11.6 %collective-permute-start = (f32[16,4096]{1,0:T(8,128)S(1)}, f32[16,4096]{1,0:T(8,128)S(1)}, u32[]{:S(2)}, u32[]{:S(2)}) collective-permute-start(f32[16,4096]{1,0:T(8,128)S(1)} %get-tuple-element.201), channel_id=1, source_target_pairs={{0,16},{16,32},{32,48},{48,64},{64,80},{80,96},{96,112},{112,128},... | collective-permute-start | bytes 786440 | tf_op jit(solution)/shard_map/while/body/eval_jaxpr/ppermute | solution.py:9
  540.1 11.6 %collective-permute-start = (f32[16,4096]{1,0:T(8,128)S(1)}, f32[16,4096]{1,0:T(8,128)S(1)}, u32[]{:S(2)}, u32[]{:S(2)}) collective-permute-start(f32[16,4096]{1,0:T(8,128)S(1)} %get-tuple-element.201), channel_id=1, source_target_pairs={{0,16},{16,32},{32,48},{48,64},{64,80},{80,96},{96,112},{112,128},... | collective-permute-start | bytes 786440 | tf_op jit(solution)/shard_map/while/body/eval_jaxpr/ppermute | solution.py:9
  552.2 11.6 %collective-permute-start = (f32[16,4096]{1,0:T(8,128)S(1)}, f32[16,4096]{1,0:T(8,128)S(1)}, u32[]{:S(2)}, u32[]{:S(2)}) collective-permute-start(f32[16,4096]{1,0:T(8,128)S(1)} %get-tuple-element.201), channel_id=1, source_target_pairs={{0,16},{16,32},{32,48},{48,64},{64,80},{80,96},{96,112},{112,128},... | collective-permute-start | bytes 786440 | tf_op jit(solution)/shard_map/while/body/eval_jaxpr/ppermute | solution.py:9
